TPU v7x, 128 devices: a whole 4x4x4 slice. The times are simulated.
128 devices in a mesh: vocab: 8 (over x_lo, y), dp: 8 (over z, core), teacher: 2 (over x_hi).
Axes of the slice: x: 4 (x_hi: 2, x_lo: 2; x = x_hi * 2 + x_lo), y: 4, z: 4, core: 2. Of those that a mesh axis runs over, the one named last changes fastest.
Arguments:
- hidden_states: bfloat16 [2048, 4096], P('teacher'), may hold values from -300 to 300
- head_weight: bfloat16 [4096, 65536], P(None, ('vocab', 'dp')), may hold values from -3 to 3
- teacher_logits: bfloat16 [2048, 65536], P(None, ('vocab', 'dp', 'teacher')), may hold values from -20 to 460
- token_weight: float32 [2048], P('teacher'), may hold values from 2 to 20
Outputs:
- hidden_grad: bfloat16 [2048, 4096], P('teacher', ('vocab', 'dp'))
- weight_grad: bfloat16 [4096, 65536], P('teacher', ('vocab', 'dp'))
All inputs are finite; a program needn't handle non-finite values.
Results may differ from a plain program's by a relative error of at most 0.005.
Values may be sent and summed in bfloat16 or wider, within the bound.
No kernel may reach another device: no remote copies, remote signals or barrier semaphores. Data moves between devices by JAX's collectives and lax.ppermute only.
A program may use at most 192 MiB of HBM per device.

v0:
```python
import jax
import jax.numpy as jnp
from jax import lax
from jax.sharding import PartitionSpec as P


def per_device(hidden_states, head_weight, teacher_logits, token_weight):
    teacher = lax.all_to_all(
        teacher_logits, "teacher", split_axis=0, concat_axis=1, tiled=True
    ).astype(jnp.float32)
    logits = jnp.dot(hidden_states, head_weight, preferred_element_type=jnp.float32)
    student_top = jnp.max(logits, axis=1)
    teacher_top = jnp.max(teacher, axis=1)
    student_top, teacher_top = lax.pmax((student_top, teacher_top), ("vocab", "dp"))
    student_total = jnp.sum(jnp.exp(logits - student_top[:, None]), axis=1)
    teacher_total = jnp.sum(jnp.exp(teacher - teacher_top[:, None]), axis=1)
    student_total, teacher_total = lax.psum((student_total, teacher_total), ("vocab", "dp"))
    student_norm = student_top + jnp.log(student_total)
    teacher_norm = teacher_top + jnp.log(teacher_total)
    logit_grad = (
        token_weight[:, None]
        * (jnp.exp(logits - student_norm[:, None]) - jnp.exp(teacher - teacher_norm[:, None]))
    ).astype(jnp.bfloat16)
    hidden_share = lax.psum_scatter(
        lax.dot_general(
            head_weight, logit_grad, (((1,), (1,)), ((), ())), preferred_element_type=jnp.float32
        ),
        ("vocab", "dp"),
        scatter_dimension=0,
        tiled=True,
    )
    hidden_grad = hidden_share.T.astype(jnp.bfloat16)
    weight_share = lax.psum_scatter(
        lax.dot_general(
            hidden_states, logit_grad, (((0,), (0,)), ((), ())), preferred_element_type=jnp.float32
        ),
        "teacher",
        scatter_dimension=0,
        tiled=True,
    )
    return (hidden_grad, weight_share.astype(jnp.bfloat16))


def solution(mesh):
    return jax.shard_map(
        per_device,
        mesh=mesh,
        in_specs=(
            P("teacher", None),
            P(None, ("vocab", "dp")),
            P(None, ("vocab", "dp", "teacher")),
            P("teacher"),
        ),
        out_specs=(P("teacher", ("vocab", "dp")), P("teacher", ("vocab", "dp"))),
        check_vma=False,
    )
```

profile of v0, /device:TPU:1, one launch (start us, length us, event | category | flops | bytes accessed | tf_op | source)
XLA Modules:
  0.0 890.2 jit_solution(3435739700118504908)
XLA Ops:
  7.2 4.0 copy.9
  11.1 4.8 all-to-all-start
  16.0 15.1 %fusion.4 = (f32[1024]{0:T(1024)S(1)}, f32[1024,1024]{0,1:T(8,128)}) fusion(bf16[1024,4096]{1,0:T(8,128)(2,1)} %param.4, bf16[4096,1024]{1,0:T(8,128)(2,1)} %param.5), kind=kOutput, calls=%fused_computation.12 | convolution fusion | flops 8590982144 | bytes 20975616 | tf_op jit(solution)/shard_map/dot_general | solution.py:11
  31.1 10.4 %all-to-all-done = bf16[2,1024,512]{1,2,0:T(8,128)(2,1)S(1)} async-done(((bf16[2,1024,512]{1,2,0:T(8,128)(2,1)}), bf16[2,1024,512]{1,2,0:T(8,128)(2,1)S(1)}, u32[]{:S(2)}, u32[]{:S(2)}) %all-to-all-start) | async-done | bytes 2097184 | tf_op jit(solution)/shard_map/all_to_all | solution.py:8
  41.4 0.4 reduce_max.24
  41.8 142.9 %all-reduce.1 = (f32[1024]{0:T(1024)S(1)}, f32[1024]{0:T(1024)S(1)}) all-reduce(bf16[1024]{0:T(1024)(128)(2,1)S(1)} %reduce_max.24, f32[1024]{0:T(1024)S(1)} %get-tuple-element.10), channel_id=1, replica_groups=mesh['vocab'=8,'dp'=8,'teacher'=2] {'vocab','dp'}, use_global_device_ids=true, to_apply=%region_5.0 | all-reduce | flops 2048 | bytes 14336 | tf_op jit(solution)/shard_map/pmax | solution.py:14
  184.7 2.8 exponential_reduce_fusion.1
  187.6 0.7 exponential_reduce_fusion
  188.3 145.1 %all-reduce = (f32[1024]{0:T(1024)S(1)}, f32[1024]{0:T(1024)S(1)}) all-reduce(f32[1024]{0:T(1024)S(1)} %exponential_reduce_fusion, f32[1024]{0:T(1024)S(1)} %exponential_reduce_fusion.1), channel_id=1, replica_groups=mesh['vocab'=8,'dp'=8,'teacher'=2] {'vocab','dp'}, use_global_device_ids=true, to_apply=%region_7.0 | all-reduce | flops 2048 | bytes 16384 | tf_op jit(solution)/shard_map/psum | solution.py:17
  333.4 3.5 fusion.3
  336.9 1.3 copy-done
  338.2 14.5 %convolution_bitcast_fusion.1 = f32[4096,1024]{0,1:T(8,128)} fusion(bf16[1024,1024]{0,1:T(8,128)(2,1)S(1)} %fusion.3, bf16[4096,1024]{1,0:T(8,128)(2,1)} %param.5), kind=kOutput, calls=%fused_computation.1 | convolution fusion | flops 8589934592 | bytes 27262976 | tf_op jit(solution)/shard_map/dot_general | solution.py:25
  352.7 17.5 %copy.12 = f32[4096,1024]{1,0:T(8,128)} copy(f32[4096,1024]{0,1:T(8,128)} %convolution_bitcast_fusion.1) | data formatting | bytes 33554432
  370.2 0.0 reduce-scatter.7.cloned.1.call-update
  370.2 0.0 reduce-scatter.5.cloned.1.call-start
  370.2 1.5 copy-done.1
  371.8 14.5 %convolution_bitcast_fusion = f32[4096,1024]{0,1:T(8,128)} fusion(bf16[1024,1024]{0,1:T(8,128)(2,1)S(1)} %copy-done.1, bf16[1024,4096]{1,0:T(8,128)(2,1)} %param.4), kind=kOutput, calls=%fused_computation | convolution fusion | flops 8589934592 | bytes 27262976 | tf_op jit(solution)/shard_map/dot_general | solution.py:34
  386.3 0.0 reduce-scatter.5.cloned.1.call-update
  386.3 287.1 %reduce-scatter.7.cloned.1.call-done = f32[64,1024]{1,0:T(8,128)} async-done(((f32[4096,1024]{1,0:T(8,128)}), f32[64,1024]{1,0:T(8,128)}) %reduce-scatter.7.cloned.1.call-update) | async-done | bytes 262160
  673.4 1.1 copy.13
  674.6 0.8 copy.10
  675.3 195.6 %reduce-scatter.5.cloned.1.call-done = f32[2048,1024]{0,1:T(8,128)} async-done(((f32[4096,1024]{0,1:T(8,128)}), f32[2048,1024]{0,1:T(8,128)}) %reduce-scatter.5.cloned.1.call-update) | async-done | bytes 8388624 | tf_op jit(solution)/shard_map/reduce_scatter | solution.py:33
  871.0 6.0 convert_element_type.32
  876.9 6.4 copy.11
  (6 shorter events, 0.0 us)
Async XLA Ops:
  11.1 30.3 %all-to-all-start = ((bf16[2,1024,512]{1,2,0:T(8,128)(2,1)}), bf16[2,1024,512]{1,2,0:T(8,128)(2,1)S(1)}, u32[]{:S(2)}, u32[]{:S(2)}) async-start(bf16[2,1024,512]{1,2,0:T(8,128)(2,1)} %copy.9), calls=%async_computation | async-start | bytes 4194304 | tf_op jit(solution)/shard_map/all_to_all | solution.py:8
  16.0 657.5 %reduce-scatter.7.cloned.1.call-start = ((), (), s32[]{:S(2)}) async-start(), calls=%async_computation.4 | async-start | bytes 17039360
  31.1 302.3 %copy-start.2 = (f32[1024]{0:T(1024)S(1)}, f32[1024]{0:T(1024)}, u32[]{:S(2)}) copy-start(f32[1024]{0:T(1024)} %param.7) | copy-start | bytes 12292
  336.9 1.3 copy-start
  370.2 1.6 copy-start.1
  370.2 500.8 %reduce-scatter.5.cloned.1.call-start = ((), (), s32[]{:S(2)}) async-start(), calls=%async_computation.3 | async-start | bytes 25165824 | tf_op jit(solution)/shard_map/reduce_scatter | solution.py:33
Sparse Core Ops, SparseCore 0:
  370.3 303.0 reduce-scatter.6
  675.8 195.0 reduce-scatter.4
where the time goes:
time: 891 us; the launch traced here: 890 us
  waiting for transfers between devices  493 us (55%)
  blocking collectives  288 us (32%)
  matrix products  44.1 us (5%)
  local copies, waits for them, and re-layouts  32.6 us (4%)
  between operations  14.1 us (2%)
  other arithmetic  13.4 us (2%)
    unnamed x3, waiting for transfers between devices  287 us
    reduce_scatter x1, waiting for transfers between devices, per_device(): lax.psum_scatter(lax.dot_general(hidden_states, logit_grad, (((0,), (0,))...  196 us
    psum x1, blocking collectives, per_device(): lax.psum((student_total, teacher_total), ('vocab', 'dp'))  145 us
    pmax x1, blocking collectives, per_device(): lax.pmax((student_top, teacher_top), ('vocab', 'dp'))  143 us
    unnamed x10, local copies, waits for them, and re-layouts  28.6 us
  transfers between devices with their start and end apart: 3, of which 3 were waited for; matrix products, arithmetic and copies ran while one was open for 4% of the time, Pallas kernels for 0%

commit v1 on v0

--- a/solution.py
+++ b/solution.py
@@ -14,7 +14,7 @@
     student_top, teacher_top = lax.pmax((student_top, teacher_top), ("vocab", "dp"))
     student_total = jnp.sum(jnp.exp(logits - student_top[:, None]), axis=1)
     teacher_total = jnp.sum(jnp.exp(teacher - teacher_top[:, None]), axis=1)
-    student_total, teacher_total = lax.psum((student_total, teacher_total), ("vocab", "dp"))
+    student_total, teacher_total = lax.psum(lax.psum((student_total, teacher_total), "dp"), "vocab")
     student_norm = student_top + jnp.log(student_total)
     teacher_norm = teacher_top + jnp.log(teacher_total)
     logit_grad = (

time: 891 us -> 781 us (0.88)
  blocking collectives: 288 us -> 173 us
    psum x1 -> x2, blocking collectives: 145 us -> 30 us  [the longest x1 17.1 us: per_device(): lax.psum((student_total, teacher_total), 'dp')]
where the time goes in v1:
time: 781 us; the launch traced here: 780 us
  waiting for transfers between devices  498 us (64%)
  blocking collectives  173 us (22%)
  matrix products  44 us (6%)
  local copies, waits for them, and re-layouts  32.6 us (4%)
  between operations  14.1 us (2%)
  other arithmetic  13.4 us (2%)
    unnamed x3, waiting for transfers between devices  292 us
    reduce_scatter x1, waiting for transfers between devices, per_device(): lax.psum_scatter(lax.dot_general(hidden_states, logit_grad, (((0,), (0,))...  196 us
    pmax x1, blocking collectives, per_device(): lax.pmax((student_top, teacher_top), ('vocab', 'dp'))  143 us
    unnamed x10, local copies, waits for them, and re-layouts  28.6 us
    psum x1, blocking collectives, per_device(): lax.psum((student_total, teacher_total), 'dp')  17.1 us
  transfers between devices with their start and end apart: 3, of which 3 were waited for; matrix products, arithmetic and copies ran while one was open for 4% of the time, Pallas kernels for 0%

profile of v1, /device:TPU:1, one launch (start us, length us, event | category | flops | bytes accessed | tf_op | source)
XLA Modules:
  0.0 780.0 jit_solution(6962988611745767033)
XLA Ops:
  7.2 4.0 copy.9
  11.1 4.8 all-to-all-start
  16.0 15.1 %fusion.4 = (f32[1024]{0:T(1024)S(1)}, f32[1024,1024]{0,1:T(8,128)}) fusion(bf16[1024,4096]{1,0:T(8,128)(2,1)} %param.4, bf16[4096,1024]{1,0:T(8,128)(2,1)} %param.5), kind=kOutput, calls=%fused_computation.12 | convolution fusion | flops 8590982144 | bytes 20975616 | tf_op jit(solution)/shard_map/dot_general | solution.py:11
  31.1 10.4 %all-to-all-done = bf16[2,1024,512]{1,2,0:T(8,128)(2,1)S(1)} async-done(((bf16[2,1024,512]{1,2,0:T(8,128)(2,1)}), bf16[2,1024,512]{1,2,0:T(8,128)(2,1)S(1)}, u32[]{:S(2)}, u32[]{:S(2)}) %all-to-all-start) | async-done | bytes 2097184 | tf_op jit(solution)/shard_map/all_to_all | solution.py:8
  41.4 0.4 reduce_max.24
  41.8 142.9 %all-reduce = (f32[1024]{0:T(1024)S(1)}, f32[1024]{0:T(1024)S(1)}) all-reduce(bf16[1024]{0:T(1024)(128)(2,1)S(1)} %reduce_max.24, f32[1024]{0:T(1024)S(1)} %get-tuple-element.12), channel_id=1, replica_groups=mesh['vocab'=8,'dp'=8,'teacher'=2] {'vocab','dp'}, use_global_device_ids=true, to_apply=%region_6.0 | all-reduce | flops 2048 | bytes 14336 | tf_op jit(solution)/shard_map/pmax | solution.py:14
  184.7 2.8 exponential_reduce_fusion.1
  187.6 0.7 exponential_reduce_fusion
  188.3 17.1 %all-reduce.1 = (f32[1024]{0:T(1024)S(1)}, f32[1024]{0:T(1024)S(1)}) all-reduce(f32[1024]{0:T(1024)S(1)} %exponential_reduce_fusion, f32[1024]{0:T(1024)S(1)} %exponential_reduce_fusion.1), channel_id=1, replica_groups=mesh['vocab'=8,'dp'=8,'teacher'=2] {'dp'}, use_global_device_ids=true, to_apply=%region_8.0 | all-reduce | flops 2048 | bytes 16384 | tf_op jit(solution)/shard_map/psum | solution.py:17
  205.4 12.9 %all-reduce.2 = (f32[1024]{0:T(1024)S(1)}, f32[1024]{0:T(1024)S(1)}) all-reduce(f32[1024]{0:T(1024)S(1)} %get-tuple-element.8, f32[1024]{0:T(1024)S(1)} %get-tuple-element.9), channel_id=1, replica_groups=mesh['vocab'=8,'dp'=8,'teacher'=2] {'vocab'}, use_global_device_ids=true, to_apply=%region_9.0 | all-reduce | flops 2048 | bytes 16384 | tf_op jit(solution)/shard_map/psum | solution.py:17
  218.3 3.5 fusion.3
  221.8 1.3 copy-done
  223.1 14.5 %convolution_bitcast_fusion.1 = f32[4096,1024]{0,1:T(8,128)} fusion(bf16[1024,1024]{0,1:T(8,128)(2,1)S(1)} %fusion.3, bf16[4096,1024]{1,0:T(8,128)(2,1)} %param.5), kind=kOutput, calls=%fused_computation.1 | convolution fusion | flops 8589934592 | bytes 27262976 | tf_op jit(solution)/shard_map/dot_general | solution.py:25
  237.6 17.5 %copy.12 = f32[4096,1024]{1,0:T(8,128)} copy(f32[4096,1024]{0,1:T(8,128)} %convolution_bitcast_fusion.1) | data formatting | bytes 33554432
  255.1 0.0 reduce-scatter.7.cloned.1.call-update
  255.1 0.0 reduce-scatter.5.cloned.1.call-start
  255.2 1.5 copy-done.1
  256.7 14.4 %convolution_bitcast_fusion = f32[4096,1024]{0,1:T(8,128)} fusion(bf16[1024,1024]{0,1:T(8,128)(2,1)S(1)} %copy-done.1, bf16[1024,4096]{1,0:T(8,128)(2,1)} %param.4), kind=kOutput, calls=%fused_computation | convolution fusion | flops 8589934592 | bytes 27262976 | tf_op jit(solution)/shard_map/dot_general | solution.py:34
  271.1 292.2 %reduce-scatter.7.cloned.1.call-done = f32[64,1024]{1,0:T(8,128)} async-done(((f32[4096,1024]{1,0:T(8,128)}), f32[64,1024]{1,0:T(8,128)}) %reduce-scatter.7.cloned.1.call-update) | async-done | bytes 262160
  563.3 1.1 copy.13
  564.4 0.8 copy.10
  565.2 195.7 %reduce-scatter.5.cloned.1.call-done = f32[2048,1024]{0,1:T(8,128)} async-done(((f32[4096,1024]{0,1:T(8,128)}), f32[2048,1024]{0,1:T(8,128)}) %reduce-scatter.5.cloned.1.call-update) | async-done | bytes 8388624 | tf_op jit(solution)/shard_map/reduce_scatter | solution.py:33
  760.9 6.0 convert_element_type.32
  766.8 6.4 copy.11
  (7 shorter events, 0.0 us)
Async XLA Ops:
  11.1 30.3 %all-to-all-start = ((bf16[2,1024,512]{1,2,0:T(8,128)(2,1)}), bf16[2,1024,512]{1,2,0:T(8,128)(2,1)S(1)}, u32[]{:S(2)}, u32[]{:S(2)}) async-start(bf16[2,1024,512]{1,2,0:T(8,128)(2,1)} %copy.9), calls=%async_computation | async-start | bytes 4194304 | tf_op jit(solution)/shard_map/all_to_all | solution.py:8
  16.0 547.3 %reduce-scatter.7.cloned.1.call-start = ((), (), s32[]{:S(2)}) async-start(), calls=%async_computation.4 | async-start | bytes 17039360
  31.1 187.3 %copy-start.2 = (f32[1024]{0:T(1024)S(1)}, f32[1024]{0:T(1024)}, u32[]{:S(2)}) copy-start(f32[1024]{0:T(1024)} %param.7) | copy-start | bytes 12292
  221.8 1.3 copy-start
  255.1 1.6 copy-start.1
  255.1 505.7 %reduce-scatter.5.cloned.1.call-start = ((), (), s32[]{:S(2)}) async-start(), calls=%async_computation.3 | async-start | bytes 25165824 | tf_op jit(solution)/shard_map/reduce_scatter | solution.py:33
Sparse Core Ops, SparseCore 0:
  255.2 307.9 reduce-scatter.6
  565.7 195.1 reduce-scatter.4
